TPU v7x, 32 devices: a whole 2x2x4 slice. The times are simulated.
32 devices in a mesh: layer: 4 (over x, core), feat: 8 (over z, y).
Axes of the slice: x: 2, y: 2, z: 4, core: 2. Of those that a mesh axis runs over, the one named last changes fastest.
Arguments:
- gradient: bfloat16 [4, 2560, 2560], P('layer', 'feat'), may hold values from -3 to 3
- in_inverse: bfloat16 [4, 2560, 2560], P('layer', 'feat'), may hold values from -1 to 2.5, as said below
- in_coupling: bfloat16 [4, 2560, 2560], P('layer', 'feat'), may hold values from -0.125 to 0.125
- in_carry: bfloat16 [4, 2560, 2560], P('layer', 'feat'), may hold values from -0.125 to 0.125
- out_inverse: bfloat16 [4, 20, 128, 128], P('layer'), may hold values from -1 to 2.5, as said below
- out_coupling: bfloat16 [4, 20, 128, 128], P('layer'), may hold values from -0.5 to 0.5
Outputs:
- update: bfloat16 [4, 2560, 2560], P('layer', 'feat')
Inputs may be any that keep to these rules, and one draw needn't show every extreme that they name: `in_inverse`: symmetric in its last two dimensions. `out_inverse`: symmetric in its last two dimensions.
All inputs are finite; a program needn't handle non-finite values.
Results may differ from a plain program's by a relative error of at most 0.006.
Values may be sent and summed in bfloat16 or wider, within the bound.
A program may use at most 64 MiB of HBM per device.

v0:
```python
import jax
import jax.numpy as jnp
from jax import lax
from jax.sharding import PartitionSpec as P


def from_behind(x, axis, by):
    size = lax.axis_size(axis)
    pairs = [(i, i + by) for i in range(size) if 0 <= i + by < size]
    return lax.ppermute(x, axis, pairs)


def block_apply(matrix, table, flipped):
    row_count = matrix.shape[0]
    blocks = table.shape[0]
    block_width = table.shape[1]
    grouped = matrix.reshape(row_count, blocks, block_width)
    pattern = "rnb,ncb->rnc" if flipped else "rnb,nbc->rnc"
    product = jnp.einsum(pattern, grouped, table, preferred_element_type=jnp.float32)
    return product.reshape(row_count, blocks * block_width)


def contract_rows(factor, piece):
    return jnp.dot(factor, piece, preferred_element_type=jnp.float32)


def local(gradient, in_inverse, in_coupling, in_carry, out_inverse, out_coupling):
    grad_rows = gradient[0]
    inverse_rows = in_inverse[0]
    coupling_rows = in_coupling[0]
    carry_rows = in_carry[0]
    out_inv = out_inverse[0]
    out_psi = out_coupling[0]
    psi_from_below = from_behind(out_psi, "layer", 1)
    from_above = from_behind(grad_rows, "layer", -1)
    near_rows = block_apply(from_above, out_psi, True).astype(jnp.bfloat16)
    coupled = contract_rows(coupling_rows, lax.all_gather(near_rows, "feat", axis=0, tiled=True))
    reduced = (grad_rows.astype(jnp.float32) - coupled).astype(jnp.bfloat16)
    piece = lax.all_gather(reduced, "feat", axis=0, tiled=True)
    whitened_acc = contract_rows(inverse_rows, piece)
    carried_acc = contract_rows(carry_rows, piece)
    whitened = whitened_acc.astype(jnp.bfloat16)
    carried = carried_acc.astype(jnp.bfloat16)
    local_term = block_apply(whitened, out_inv, False)
    middle = block_apply(carried, out_inv, False).astype(jnp.bfloat16)
    middle_from_below = from_behind(middle, "layer", 1)
    incoming = block_apply(middle_from_below, psi_from_below, False)
    return (local_term - incoming).astype(jnp.bfloat16)[None]


def solution(mesh):
    return jax.shard_map(
        local,
        mesh=mesh,
        in_specs=(
            P("layer", "feat", None),
            P("layer", "feat", None),
            P("layer", "feat", None),
            P("layer", "feat", None),
            P("layer", None, None, None),
            P("layer", None, None, None),
        ),
        out_specs=P("layer", "feat", None),
        check_vma=False,
    )
```

profile of v0, /device:TPU:5, one launch (start us, length us, event | category | flops | bytes accessed | tf_op | source)
XLA Modules:
  0.0 458.3 jit_solution(10141382669554686572)
XLA Ops:
  6.5 2.7 collective-permute-start
  9.3 20.1 %collective-permute-done = bf16[320,2560]{1,0:T(8,128)(2,1)S(1)} collective-permute-done((bf16[320,2560]{1,0:T(8,128)(2,1)}, bf16[320,2560]{1,0:T(8,128)(2,1)S(1)}, u32[]{:S(2)}, u32[]{:S(2)}) %collective-permute-start) | collective-permute-done | bytes 1638432 | tf_op jit(solution)/shard_map/ppermute | solution.py:10
  29.3 1.7 fusion.14
  31.0 1.4 copy.47
  32.5 0.0 all-gather.3.cloned.1.call-update
  32.5 0.0 all-gather.5.cloned.1.call-start
  32.6 180.7 %all-gather.3.cloned.1.call-done = bf16[2560,2560]{1,0:T(8,128)(2,1)} async-done(((bf16[320,2560]{1,0:T(8,128)(2,1)}), bf16[2560,2560]{1,0:T(8,128)(2,1)}) %all-gather.3.cloned.1.call-update) | async-done | bytes 13107216 | tf_op jit(solution)/shard_map/all_gather | solution.py:37
  213.3 10.2 %fusion.1 = bf16[320,2560]{1,0:T(8,128)(2,1)} fusion(bf16[2560,2560]{1,0:T(8,128)(2,1)} %all-gather.3.cloned.1.call-done, bf16[1,320,2560]{2,1,0:T(8,128)(2,1)S(1)} %copy-done, bf16[1,320,2560]{2,1,0:T(8,128)(2,1)S(1)} %copy-done.4), kind=kOutput, calls=%fused_computation.2 | convolution fusion | flops 4196761600 | bytes 18022400 | tf_op jit(solution)/shard_map/dot_general | solution.py:24
  223.5 0.0 all-gather.5.cloned.1.call-update
  223.5 0.0 copy-start.1
  223.5 180.8 %all-gather.5.cloned.1.call-done = bf16[2560,2560]{1,0:T(8,128)(2,1)} async-done(((bf16[320,2560]{1,0:T(8,128)(2,1)}), bf16[2560,2560]{1,0:T(8,128)(2,1)}) %all-gather.5.cloned.1.call-update) | async-done | bytes 13107216 | tf_op jit(solution)/shard_map/all_gather | solution.py:39
  404.3 9.7 %fusion.26 = bf16[40,20,8,128]{3,2,1,0:T(8,128)(2,1)S(1)} fusion(bf16[2560,2560]{1,0:T(8,128)(2,1)} %all-gather.5.cloned.1.call-done, bf16[1,320,2560]{2,1,0:T(8,128)(2,1)} %param.9), kind=kOutput, calls=%fused_computation.26 | convolution fusion | flops 4195123200 | bytes 16384000 | tf_op jit(solution)/shard_map/dot_general | solution.py:24
  414.1 0.6 fusion.17
  414.7 0.0 copy-start.2
  414.7 0.0 copy-start.5
  414.7 0.3 copy.46
  415.0 4.5 collective-permute-start.1
  419.5 1.9 collective-permute-start.2
  421.5 4.4 fusion.23
  425.8 0.6 fusion.6
  426.4 18.1 %collective-permute-done.2 = bf16[20,128,128]{2,1,0:T(8,128)(2,1)S(1)} collective-permute-done((bf16[20,128,128]{2,1,0:T(8,128)(2,1)S(1)}, bf16[20,128,128]{2,1,0:T(8,128)(2,1)S(1)}, u32[]{:S(2)}, u32[]{:S(2)}) %collective-permute-start.2) | collective-permute-done | bytes 655392 | tf_op jit(solution)/shard_map/ppermute | solution.py:10
  444.6 0.6 fusion.20
  445.2 2.4 copy.15
  447.6 3.9 convert_element_type.66
  (11 shorter events, 0.0 us)
Async XLA Ops:
  6.5 206.7 %copy-start = (bf16[1,320,2560]{2,1,0:T(8,128)(2,1)S(1)}, bf16[1,320,2560]{2,1,0:T(8,128)(2,1)}, u32[]{:S(2)}) copy-start(bf16[1,320,2560]{2,1,0:T(8,128)(2,1)} %param.8) | copy-start | bytes 4915204
  6.5 206.7 %all-gather.3.cloned.1.call-start = ((), (), s32[]{:S(2)}) async-start(), calls=%async_computation | async-start | bytes 14745600 | tf_op jit(solution)/shard_map/all_gather | solution.py:37
  6.5 22.8 %collective-permute-start = (bf16[320,2560]{1,0:T(8,128)(2,1)}, bf16[320,2560]{1,0:T(8,128)(2,1)S(1)}, u32[]{:S(2)}, u32[]{:S(2)}) collective-permute-start(bf16[320,2560]{1,0:T(8,128)(2,1)} %bitcast.82), channel_id=1, source_target_pairs={{8,0},{16,8},{24,16},{9,1},{17,9},{25,17},{10,2},{18,10},{26,18},{... | collective-permute-start | bytes 4915208 | tf_op jit(solution)/shard_map/ppermute | solution.py:10
  32.5 180.8 %copy-start.4 = (bf16[1,320,2560]{2,1,0:T(8,128)(2,1)S(1)}, bf16[1,320,2560]{2,1,0:T(8,128)(2,1)}, u32[]{:S(2)}) copy-start(bf16[1,320,2560]{2,1,0:T(8,128)(2,1)} %param.6) | copy-start | bytes 4915204
  32.5 371.8 %all-gather.5.cloned.1.call-start = ((), (), s32[]{:S(2)}) async-start(), calls=%async_computation.1 | async-start | bytes 14745600 | tf_op jit(solution)/shard_map/all_gather | solution.py:39
  223.5 190.6 %copy-start.1 = (bf16[1,20,128,128]{3,2,1,0:T(8,128)(2,1)S(1)}, bf16[1,20,128,128]{3,2,1,0:T(8,128)(2,1)}, u32[]{:S(2)}) copy-start(bf16[1,20,128,128]{3,2,1,0:T(8,128)(2,1)} %param.10) | copy-start | bytes 1966084
  404.3 17.1 %copy-start.3 = (bf16[2560,2560]{1,0:T(8,128)(2,1)S(1)}, bf16[2560,2560]{1,0:T(8,128)(2,1)}, u32[]{:S(2)}) copy-start(bf16[2560,2560]{1,0:T(8,128)(2,1)} %all-gather.5.cloned.1.call-done) | copy-start | bytes 39321604
  414.7 4.8 %copy-start.2 = (bf16[1,20,128,128]{3,2,1,0:T(8,128)(2,1)S(1)}, bf16[1,20,128,128]{3,2,1,0:T(8,128)(2,1)}, u32[]{:S(2)}) copy-start(bf16[1,20,128,128]{3,2,1,0:T(8,128)(2,1)} %param.11) | copy-start | bytes 1966084
  414.7 6.8 %copy-start.5 = (bf16[1,320,2560]{2,1,0:T(8,128)(2,1)S(1)}, bf16[1,320,2560]{2,1,0:T(8,128)(2,1)}, u32[]{:S(2)}) copy-start(bf16[1,320,2560]{2,1,0:T(8,128)(2,1)} %param.7) | copy-start | bytes 4915204
  415.0 29.6 %collective-permute-start.1 = (bf16[320,2560]{1,0:T(8,128)(2,1)S(1)}, bf16[320,2560]{1,0:T(8,128)(2,1)S(1)}, u32[]{:S(2)}, u32[]{:S(2)}) collective-permute-start(bf16[320,2560]{1,0:T(8,128)(2,1)S(1)} %bitcast.80), channel_id=1, source_target_pairs={{0,8},{8,16},{16,24},{1,9},{9,17},{17,25},{2,10},{10,18},{18,26},{... | collective-permute-start | bytes 4915208 | tf_op jit(solution)/shard_map/ppermute | solution.py:10
  419.5 25.1 %collective-permute-start.2 = (bf16[20,128,128]{2,1,0:T(8,128)(2,1)S(1)}, bf16[20,128,128]{2,1,0:T(8,128)(2,1)S(1)}, u32[]{:S(2)}, u32[]{:S(2)}) collective-permute-start(bf16[20,128,128]{2,1,0:T(8,128)(2,1)S(1)} %bitcast.81), channel_id=1, source_target_pairs={{0,8},{8,16},{16,24},{1,9},{9,17},{17,25},{2,10},{10,18},{18,26},{... | collective-permute-start | bytes 1966088 | tf_op jit(solution)/shard_map/ppermute | solution.py:10
Sparse Core Ops, SparseCore 0:
  32.6 180.5 all-gather.2
  223.6 180.6 all-gather.4
where the time goes:
time: 460 us; the launch traced here: 458 us
  waiting for transfers between devices  400 us (87%)
  matrix products  27.8 us (6%)
  between operations  13.5 us (3%)
  starting transfers between devices  9.17 us (2%)
  local copies, waits for them, and re-layouts  8.05 us (2%)
    all_gather x1, waiting for transfers between devices, local(): piece = lax.all_gather(reduced, 'feat', axis=0, tiled=True)  181 us
    all_gather x1, waiting for transfers between devices, local(): lax.all_gather(near_rows, 'feat', axis=0, tiled=True)  181 us
    ppermute x3, waiting for transfers between devices, from_behind(): return lax.ppermute(x, axis, pairs)  38.2 us
    dot_general x3, matrix products, contract_rows(): return jnp.dot(factor, piece, preferred_element_type=jnp.float32)  24.3 us
  transfers between devices with their start and end apart: 5, of which 4 were waited for; matrix products, arithmetic and copies ran while one was open for 1% of the time, Pallas kernels for 0%

commit v1 on v0

v1 whole, which is shorter than its diff:
```python
import functools

import jax
import jax.numpy as jnp
from jax import lax
from jax.experimental import pallas as pl
from jax.experimental.pallas import tpu as pltpu
from jax.sharding import PartitionSpec as P

MESH = pl.DeviceIdType.MESH
BF = jnp.bfloat16
F32 = jnp.float32


def kernel(nl, nb, nch, g_ref, s_ref, c_ref, k_ref, oi_ref, ps_ref, out_ref,
           w, gl, gn, tab, n_all, r_all, l_st, p_st, l_in, p_in,
           w_recv, w_send, w_fwd, gl_recv, gl_send, gn_recv, gn_send, t_recv, t_send,
           n_recv, n_send, r_recv, r_send, l_recv, l_send, p_recv, p_send):
    r, d = out_ref.shape
    h = d // 2
    cw = h // nch
    blk = ps_ref.shape[1]
    hb = ps_ref.shape[0] // 2
    per = cw // blk
    l = lax.axis_index("layer")
    f = lax.axis_index("feat")
    a, c = l // 2, l % 2
    b, p = f // 2, f % 2
    role = 2 * a + p
    home = c == p
    away = c != p
    chained = role < nl - 1
    core_mate = (2 * a + 1 - c, f)
    swap_mate = (l, 2 * b + 1 - p)

    def remote(src, dst, ss, rs, dev):
        return pltpu.make_async_remote_copy(
            src_ref=src, dst_ref=dst, send_sem=ss, recv_sem=rs,
            device_id=dev, device_id_type=MESH)

    def arrived(dst, sem):
        pltpu.make_async_copy(dst, dst, sem).wait()

    barrier = pltpu.get_barrier_semaphore()
    for dl in range(1, nl):
        for q in range(2):
            pl.semaphore_signal(barrier, inc=1, device_id=(lax.rem(l + dl, nl), 2 * b + q), device_id_type=MESH)
    pl.semaphore_signal(barrier, inc=1, device_id=swap_mate, device_id_type=MESH)

    @pl.when(b > 0)
    def _():
        pl.semaphore_signal(barrier, inc=1, device_id=(l, f - 2), device_id_type=MESH)

    @pl.when(b < nb - 1)
    def _():
        pl.semaphore_signal(barrier, inc=1, device_id=(l, f + 2), device_id_type=MESH)

    peers = 2 * nl - 1 + jnp.where(b > 0, 1, 0) + jnp.where(b < nb - 1, 1, 0)
    pl.semaphore_wait(barrier, peers)

    low = l + nl - 1
    low_a, low_p = (low - nl) // 2, lax.rem(low, 2)
    for hh in range(2):
        own = (l >= 1) & (c == 1) & (p == 0) & (c == hh)

        @pl.when(own)
        def _():
            pltpu.make_async_copy(g_ref.at[:, pl.ds(hh * h, h)], gn.at[p], gn_recv.at[p]).start()

        @pl.when((l >= 1) & jnp.logical_not(own))
        def _():
            remote(g_ref.at[:, pl.ds(hh * h, h)], gn.at[p], gn_send.at[hh], gn_recv.at[p],
                   (2 * low_a + hh, 2 * b + low_p)).start()

    @pl.when(home)
    def _():
        pltpu.make_async_copy(ps_ref.at[pl.ds(c * hb, hb)], tab.at[0], t_recv.at[0]).start()
        pltpu.make_async_copy(oi_ref.at[pl.ds(c * hb, hb)], tab.at[1], t_recv.at[1]).start()
        remote(ps_ref.at[pl.ds((1 - c) * hb, hb)], tab.at[0], t_send.at[0], t_recv.at[0], core_mate).start()
        remote(oi_ref.at[pl.ds((1 - c) * hb, hb)], tab.at[1], t_send.at[1], t_recv.at[1], core_mate).start()

    def g_half(hh):
        return g_ref.at[:, pl.ds(pl.multiple_of(hh * h, 128), h)]

    @pl.when(home)
    def _():
        pltpu.make_async_copy(g_half(c), gl.at[p], gl_recv.at[p]).start()
        remote(g_half(1 - c), gl.at[p], gl_send.at[0], gl_recv.at[p], core_mate).start()

    @pl.when(away)
    def _():
        remote(g_half(c), gl.at[p], gl_send.at[0], gl_recv.at[p], swap_mate).start()
        remote(g_half(1 - c), gl.at[p], gl_send.at[1], gl_recv.at[p], (2 * a + 1 - c, 2 * b + 1 - p)).start()

    weights = (c_ref, s_ref, k_ref)
    for m in range(3):
        @pl.when(home)
        def _():
            pltpu.make_async_copy(weights[m], w.at[m, p], w_recv.at[m, p]).start()
            remote(weights[m], w.at[m, p], w_send.at[m], w_recv.at[m, p], core_mate).start()

        @pl.when(away)
        def _():
            remote(weights[m], w.at[m, p], w_send.at[m], w_recv.at[m, p], swap_mate).start()

    def take_weight(m):
        arrived(w.at[m, 1 - p], w_recv.at[m, 1 - p])

        @pl.when(home)
        def _():
            remote(w.at[m, 1 - p], w.at[m, 1 - p], w_fwd.at[m], w_recv.at[m, 1 - p], core_mate).start()
        arrived(w.at[m, p], w_recv.at[m, p])

    def hop(buf, k, src, up, send, recv):
        dev = (l, f + 2) if up else (l, f - 2)
        return remote(buf.at[k, src], buf.at[k, src], send.at[k, src, 0 if up else 1], recv.at[k, src], dev)

    def pass_on(buf, send, recv, live, k, j):
        ok = live & (k >= 0) & (k < nch)
        if j == 0:
            @pl.when(ok & (b < nb - 1))
            def _():
                hop(buf, k, b, True, send, recv).start()

            @pl.when(ok & (b > 0))
            def _():
                hop(buf, k, b, False, send, recv).start()
        else:
            @pl.when(ok & (b - j >= 0))
            def _():
                arrived(buf.at[k, b - j], recv.at[k, b - j])

                @pl.when(b < nb - 1)
                def _():
                    hop(buf, k, b - j, True, send, recv).start()

            @pl.when(ok & (b + j < nb))
            def _():
                arrived(buf.at[k, b + j], recv.at[k, b + j])

                @pl.when(b > 0)
                def _():
                    hop(buf, k, b + j, False, send, recv).start()

    def sent(buf, send, recv, live, k):
        for src in range(nb):
            @pl.when(live & (src <= b) & (b < nb - 1))
            def _():
                hop(buf, k, src, True, send, recv).wait_send()

            @pl.when(live & (src >= b) & (b > 0))
            def _():
                hop(buf, k, src, False, send, recv).wait_send()

    def columns(k):
        return pl.ds(pl.multiple_of(k * cw, cw), cw)

    @pl.when(chained)
    def _():
        for q in range(2):
            arrived(gn.at[q], gn_recv.at[q])
    for i in range(2):
        arrived(tab.at[i], t_recv.at[i])

    def near_step(k):
        x = gn[:, :, columns(k)].reshape(2 * r, cw)
        parts = [lax.dot_general(x[:, i * blk:(i + 1) * blk], tab[0, k * per + i],
                                 (((1,), (1,)), ((), ())), preferred_element_type=F32).astype(BF)
                 for i in range(per)]
        n_all[k, b] = jnp.concatenate(parts, axis=1)

    def reduced_step(k):
        @pl.when(k == 0)
        def _():
            for q in range(2):
                arrived(gl.at[q], gl_recv.at[q])
            take_weight(0)

        @pl.when(chained)
        def _():
            x = n_all[k].reshape(nb * 2 * r, cw)
            coupled = jnp.dot(w[0].reshape(2 * r, d), x, preferred_element_type=F32)
            g = gl[:, :, columns(k)].reshape(2 * r, cw).astype(F32)
            r_all[k, b] = (g - coupled).astype(BF)

        @pl.when(jnp.logical_not(chained))
        def _():
            r_all[k, b] = gl[:, :, columns(k)].reshape(2 * r, cw)

    def local_copy(k, q):
        return remote(l_st.at[k, q], l_in.at[k, c], l_send.at[k, q], l_recv.at[k, c], (role, 2 * b + q))

    def push_copy(k, q):
        return remote(p_st.at[k, q], p_in.at[k, c], p_send.at[k, q], p_recv.at[k, c],
                      (lax.rem(role + 1, nl), 2 * b + q))

    def stays(q, layer):
        return (l == layer) & (p == q)

    def final_step(k):
        x = r_all[k].reshape(nb * 2 * r, cw)
        white = jnp.dot(w[1].reshape(2 * r, d), x, preferred_element_type=F32).astype(BF)
        for i in range(per):
            o = jnp.dot(white[:, i * blk:(i + 1) * blk], tab[1, k * per + i], preferred_element_type=F32)
            l_st[k, :, :, i * blk:(i + 1) * blk] = o.astype(BF).reshape(2, r, blk)
        for q in range(2):
            @pl.when(stays(q, role))
            def _():
                pltpu.make_async_copy(l_st.at[k, q], l_in.at[k, c], l_recv.at[k, c]).start()

            @pl.when(jnp.logical_not(stays(q, role)))
            def _():
                local_copy(k, q).start()

        @pl.when(chained)
        def _():
            y = r_all[k].reshape(nb * 2 * r, cw)
            carried = jnp.dot(w[2].reshape(2 * r, d), y, preferred_element_type=F32).astype(BF)
            for i in range(per):
                mid = jnp.dot(carried[:, i * blk:(i + 1) * blk], tab[1, k * per + i],
                              preferred_element_type=F32).astype(BF)
                o = jnp.dot(mid, tab[0, k * per + i], preferred_element_type=F32)
                p_st[k, :, :, i * blk:(i + 1) * blk] = o.astype(BF).reshape(2, r, blk)
            for q in range(2):
                @pl.when(stays(q, role + 1))
                def _():
                    pltpu.make_async_copy(p_st.at[k, q], p_in.at[k, c], p_recv.at[k, c]).start()

                @pl.when(jnp.logical_not(stays(q, role + 1)))
                def _():
                    push_copy(k, q).start()

    def out_step(k):
        for hh in range(2):
            arrived(l_in.at[k, hh], l_recv.at[k, hh])
            dst = pl.ds(pl.multiple_of(hh * h + k * cw, cw), cw)

            @pl.when(l > 0)
            def _():
                arrived(p_in.at[k, hh], p_recv.at[k, hh])
                out_ref[:, dst] = (l_in[k, hh].astype(F32) - p_in[k, hh].astype(F32)).astype(BF)

            @pl.when(l == 0)
            def _():
                out_ref[:, dst] = l_in[k, hh]

    def inside(k):
        return (k >= 0) & (k < nch)

    n_lag = nb - 1
    r_lag = 2 * (nb - 1)

    def step(t, carry):
        @pl.when(chained & inside(t))
        def _():
            near_step(t)
        for j in range(nb):
            pass_on(n_all, n_send, n_recv, chained, t - j, j)
        kr = t - n_lag

        @pl.when(inside(kr))
        def _():
            reduced_step(kr)
        for j in range(nb):
            pass_on(r_all, r_send, r_recv, True, kr - j, j)

        @pl.when(kr == min(1, nch - 1))
        def _():
            take_weight(1)

        @pl.when(kr == min(2, nch - 1))
        def _():
            take_weight(2)
        kf = t - r_lag

        @pl.when(inside(kf))
        def _():
            final_step(kf)
        ko = kf - 1

        @pl.when(inside(ko))
        def _():
            out_step(ko)
        return carry

    lax.fori_loop(0, nch + r_lag + 1, step, 0)

    def drain(k, carry):
        sent(n_all, n_send, n_recv, chained, k)
        sent(r_all, r_send, r_recv, True, k)
        for q in range(2):
            @pl.when(jnp.logical_not(stays(q, role)))
            def _():
                local_copy(k, q).wait_send()

            @pl.when(chained & jnp.logical_not(stays(q, role + 1)))
            def _():
                push_copy(k, q).wait_send()
        return carry

    lax.fori_loop(0, nch, drain, 0)

    for hh in range(2):
        own = (l >= 1) & (c == 1) & (p == 0) & (c == hh)

        @pl.when((l >= 1) & jnp.logical_not(own))
        def _():
            remote(g_ref.at[:, pl.ds(hh * h, h)], gn.at[p], gn_send.at[hh], gn_recv.at[p],
                   (2 * low_a + hh, 2 * b + low_p)).wait_send()

    @pl.when(home)
    def _():
        for i, src in enumerate((ps_ref, oi_ref)):
            remote(src.at[pl.ds((1 - c) * hb, hb)], tab.at[i], t_send.at[i], t_recv.at[i], core_mate).wait_send()
        remote(g_half(1 - c), gl.at[p], gl_send.at[0], gl_recv.at[p], core_mate).wait_send()
        for m in range(3):
            remote(w.at[m, 1 - p], w.at[m, 1 - p], w_fwd.at[m], w_recv.at[m, 1 - p], core_mate).wait_send()

    @pl.when(away)
    def _():
        remote(g_half(c), gl.at[p], gl_send.at[0], gl_recv.at[p], swap_mate).wait_send()
        remote(g_half(1 - c), gl.at[p], gl_send.at[1], gl_recv.at[p], swap_mate).wait_send()
    for m in range(3):
        remote(weights[m], w.at[m, p], w_send.at[m], w_recv.at[m, p], core_mate).wait_send()


def local(nl, nf, gradient, in_inverse, in_coupling, in_carry, out_inverse, out_coupling):
    g = gradient[0]
    r, d = g.shape
    nb = nf // 2
    blocks, blk = out_inverse.shape[1], out_inverse.shape[2]
    h = d // 2
    hb = blocks // 2
    nch = hb // 2 if hb % 2 == 0 else hb
    cw = h // nch
    dma = pltpu.SemaphoreType.DMA
    vm = pltpu.VMEM
    anyspec = pl.BlockSpec(memory_space=pl.ANY)
    out = pl.pallas_call(
        functools.partial(kernel, nl, nb, nch),
        out_shape=jax.ShapeDtypeStruct((r, d), BF),
        in_specs=[anyspec] * 6,
        out_specs=pl.BlockSpec(memory_space=pltpu.VMEM),
        scratch_shapes=[
            vm((3, 2, r, d), BF), vm((2, r, h), BF), vm((2, r, h), BF), vm((2, hb, blk, blk), BF),
            vm((nch, nb, 2 * r, cw), BF), vm((nch, nb, 2 * r, cw), BF),
            vm((nch, 2, r, cw), BF), vm((nch, 2, r, cw), BF), vm((nch, 2, r, cw), BF), vm((nch, 2, r, cw), BF),
            dma((3, 2)), dma((3,)), dma((3,)), dma((2,)), dma((2,)), dma((2,)), dma((2,)), dma((2,)), dma((2,)),
            dma((nch, nb)), dma((nch, nb, 2)), dma((nch, nb)), dma((nch, nb, 2)),
            dma((nch, 2)), dma((nch, 2)), dma((nch, 2)), dma((nch, 2)),
        ],
        compiler_params=pltpu.CompilerParams(
            collective_id=0, has_side_effects=True, vmem_limit_bytes=62 * 1024 * 1024),
    )(g, in_inverse[0], in_coupling[0], in_carry[0], out_inverse[0], out_coupling[0])
    return out[None]


def solution(mesh):
    return jax.shard_map(
        functools.partial(local, mesh.shape["layer"], mesh.shape["feat"]),
        mesh=mesh,
        in_specs=(
            P("layer", "feat", None),
            P("layer", "feat", None),
            P("layer", "feat", None),
            P("layer", "feat", None),
            P("layer", None, None, None),
            P("layer", None, None, None),
        ),
        out_specs=P("layer", "feat", None),
        check_vma=False,
    )
```

time: 460 us -> 247 us (0.54)
  waiting for transfers between devices: 400 us -> 0 us
  Pallas kernels: 0 us -> 244 us
  matrix products: 27.8 us -> 0 us
  between operations: 13.5 us -> 0.01 us
  starting transfers between devices: 9.17 us -> 0 us
  local copies, waits for them, and re-layouts: 8.05 us -> 2.7 us
    all_gather x2 -> x0, waiting for transfers between devices: 362 us -> none  [the longest x1 181 us: local(): piece = lax.all_gather(reduced, 'feat', axis=0, tiled=True)]
    pallas_call x0 -> x1, Pallas kernels: none -> 244 us  [local(): pl.pallas_call(functools.partial(kernel, nl, nb, nch), out_shape=jax.Shap...]
    ppermute x3 -> x0, waiting for transfers between devices: 38.2 us -> none  [from_behind(): return lax.ppermute(x, axis, pairs)]
    dot_general x7 -> x0, matrix products: 27.8 us -> none  [the longest x3 24.3 us: contract_rows(): return jnp.dot(factor, piece, preferred_element_type=jnp.float32)]
    ppermute x3 -> x0, starting transfers between devices: 9.13 us -> none  [from_behind(): return lax.ppermute(x, axis, pairs)]
    convert_element_type x4 -> x0, local copies, waits for them, and re-layouts: 8.02 us -> none  [the longest x2 6.29 us: local(): return (local_term - incoming).astype(jnp.bfloat16)[None]]
  transfers between devices with their start and end apart: 5 -> 0, of which waited for: 4 -> 0; matrix products, arithmetic and copies ran while one was open for 1% -> 0% of each run, Pallas kernels for 0% -> 0%
where the time goes in v1:
time: 247 us
  Pallas kernels  244 us (99%)
  local copies, waits for them, and re-layouts  2.7 us (1%)
    pallas_call x1, Pallas kernels, local(): pl.pallas_call(functools.partial(kernel, nl, nb, nch), out_shape=jax.Shap...  244 us

profile of v1, /device:TPU:5, one launch (start us, length us, event | category | flops | bytes accessed | tf_op | source)
XLA Modules:
  0.0 247.1 jit_solution(2206890561146468123)
XLA Ops:
  0.0 244.4 %shard_map.64 = bf16[320,2560]{1,0:T(8,128)(2,1)} custom-call(bf16[320,2560]{1,0:T(8,128)(2,1)} %bitcast.8, bf16[320,2560]{1,0:T(8,128)(2,1)} %bitcast.9, bf16[320,2560]{1,0:T(8,128)(2,1)} %bitcast.10, bf16[320,2560]{1,0:T(8,128)(2,1)} %bitcast.11, bf16[20,128,128]{2,1,0:T(8,128)(2,1)} %bitcast.12, bf16[20,128,128]{2,1,0:T(8,128)(2,1)} %bitcast.13), custom_call_target="tpu_custom_call" | custom-call | tf_op jit(solution)/shard_map/pallas_call | solution.py:339
  244.4 2.7 %copy.8 = bf16[1,320,2560]{2,1,0:T(8,128)(2,1)} copy(bf16[1,320,2560]{2,1,0:T(8,128)(2,1)} %bitcast.7) | data formatting | bytes 3276800

commit v2 on v1

--- a/solution.py
+++ b/solution.py
@@ -60,17 +60,29 @@
 
     low = l + nl - 1
     low_a, low_p = (low - nl) // 2, lax.rem(low, 2)
-    for hh in range(2):
-        own = (l >= 1) & (c == 1) & (p == 0) & (c == hh)
-
-        @pl.when(own)
-        def _():
-            pltpu.make_async_copy(g_ref.at[:, pl.ds(hh * h, h)], gn.at[p], gn_recv.at[p]).start()
-
-        @pl.when((l >= 1) & jnp.logical_not(own))
-        def _():
-            remote(g_ref.at[:, pl.ds(hh * h, h)], gn.at[p], gn_send.at[hh], gn_recv.at[p],
-                   (2 * low_a + hh, 2 * b + low_p)).start()
+
+    def above_cols(hh, k):
+        return g_ref.at[:, pl.ds(pl.multiple_of(hh * h + k * cw, cw), cw)]
+
+    def above_stays(hh):
+        return (l >= 1) & (c == 1) & (p == 0) & (c == hh)
+
+    def above_copy(hh, k):
+        return remote(above_cols(hh, k), gn.at[k, p], gn_send.at[k, hh], gn_recv.at[k, p],
+                      (2 * low_a + hh, 2 * b + low_p))
+
+    def send_above(k, carry):
+        for hh in range(2):
+            @pl.when(above_stays(hh))
+            def _():
+                pltpu.make_async_copy(above_cols(hh, k), gn.at[k, p], gn_recv.at[k, p]).start()
+
+            @pl.when((l >= 1) & jnp.logical_not(above_stays(hh)))
+            def _():
+                above_copy(hh, k).start()
+        return carry
+
+    lax.fori_loop(0, nch, send_above, 0)
 
     @pl.when(home)
     def _():
@@ -155,15 +167,13 @@
     def columns(k):
         return pl.ds(pl.multiple_of(k * cw, cw), cw)
 
-    @pl.when(chained)
-    def _():
-        for q in range(2):
-            arrived(gn.at[q], gn_recv.at[q])
     for i in range(2):
         arrived(tab.at[i], t_recv.at[i])
 
     def near_step(k):
-        x = gn[:, :, columns(k)].reshape(2 * r, cw)
+        for q in range(2):
+            arrived(gn.at[k, q], gn_recv.at[k, q])
+        x = gn[k].reshape(2 * r, cw)
         parts = [lax.dot_general(x[:, i * blk:(i + 1) * blk], tab[0, k * per + i],
                                  (((1,), (1,)), ((), ())), preferred_element_type=F32).astype(BF)
                  for i in range(per)]
@@ -289,6 +299,10 @@
         sent(n_all, n_send, n_recv, chained, k)
         sent(r_all, r_send, r_recv, True, k)
         for q in range(2):
+            @pl.when((l >= 1) & jnp.logical_not(above_stays(q)))
+            def _():
+                above_copy(q, k).wait_send()
+
             @pl.when(jnp.logical_not(stays(q, role)))
             def _():
                 local_copy(k, q).wait_send()
@@ -299,14 +313,6 @@
         return carry
 
     lax.fori_loop(0, nch, drain, 0)
-
-    for hh in range(2):
-        own = (l >= 1) & (c == 1) & (p == 0) & (c == hh)
-
-        @pl.when((l >= 1) & jnp.logical_not(own))
-        def _():
-            remote(g_ref.at[:, pl.ds(hh * h, h)], gn.at[p], gn_send.at[hh], gn_recv.at[p],
-                   (2 * low_a + hh, 2 * b + low_p)).wait_send()
 
     @pl.when(home)
     def _():
@@ -342,10 +348,10 @@
         in_specs=[anyspec] * 6,
         out_specs=pl.BlockSpec(memory_space=pltpu.VMEM),
         scratch_shapes=[
-            vm((3, 2, r, d), BF), vm((2, r, h), BF), vm((2, r, h), BF), vm((2, hb, blk, blk), BF),
+            vm((3, 2, r, d), BF), vm((2, r, h), BF), vm((nch, 2, r, cw), BF), vm((2, hb, blk, blk), BF),
             vm((nch, nb, 2 * r, cw), BF), vm((nch, nb, 2 * r, cw), BF),
             vm((nch, 2, r, cw), BF), vm((nch, 2, r, cw), BF), vm((nch, 2, r, cw), BF), vm((nch, 2, r, cw), BF),
-            dma((3, 2)), dma((3,)), dma((3,)), dma((2,)), dma((2,)), dma((2,)), dma((2,)), dma((2,)), dma((2,)),
+            dma((3, 2)), dma((3,)), dma((3,)), dma((2,)), dma((2,)), dma((nch, 2)), dma((nch, 2)), dma((2,)), dma((2,)),
             dma((nch, nb)), dma((nch, nb, 2)), dma((nch, nb)), dma((nch, nb, 2)),
             dma((nch, 2)), dma((nch, 2)), dma((nch, 2)), dma((nch, 2)),
         ],

time: 247 us -> 238 us (0.964)
  Pallas kernels: 244 us -> 234 us
    pallas_call x1, Pallas kernels: 244 us -> 234 us  [local(): pl.pallas_call(functools.partial(kernel, nl, nb, nch), out_shape=jax.Shap...]
where the time goes in v2:
time: 238 us; the launch traced here: 237 us
  Pallas kernels  234 us (98%)
  local copies, waits for them, and re-layouts  2.7 us (1%)
    pallas_call x1, Pallas kernels, local(): pl.pallas_call(functools.partial(kernel, nl, nb, nch), out_shape=jax.Shap...  234 us

profile of v2, /device:TPU:5, one launch (start us, length us, event | category | flops | bytes accessed | tf_op | source)
XLA Modules:
  0.0 236.5 jit_solution(16744750607295766447)
XLA Ops:
  0.0 233.8 %shard_map.64 = bf16[320,2560]{1,0:T(8,128)(2,1)} custom-call(bf16[320,2560]{1,0:T(8,128)(2,1)} %bitcast.8, bf16[320,2560]{1,0:T(8,128)(2,1)} %bitcast.9, bf16[320,2560]{1,0:T(8,128)(2,1)} %bitcast.10, bf16[320,2560]{1,0:T(8,128)(2,1)} %bitcast.11, bf16[20,128,128]{2,1,0:T(8,128)(2,1)} %bitcast.12, bf16[20,128,128]{2,1,0:T(8,128)(2,1)} %bitcast.13), custom_call_target="tpu_custom_call" | custom-call | tf_op jit(solution)/shard_map/pallas_call | solution.py:345
  233.8 2.7 %copy.8 = bf16[1,320,2560]{2,1,0:T(8,128)(2,1)} copy(bf16[1,320,2560]{2,1,0:T(8,128)(2,1)} %bitcast.7) | data formatting | bytes 3276800

commit v3 on v2

--- a/solution.py
+++ b/solution.py
@@ -12,10 +12,11 @@
 F32 = jnp.float32
 
 
-def kernel(nl, nb, nch, g_ref, s_ref, c_ref, k_ref, oi_ref, ps_ref, out_ref,
-           w, gl, gn, tab, n_all, r_all, l_st, p_st, l_in, p_in,
+def kernel(nl, nb, nch, lent, g_ref, s_ref, c_ref, k_ref, oi_ref, ps_ref, out_ref,
+           w, gl, gn, tab, n_all, r_all, l_st, p_st, l_in, p_in, w2, gl2, gn2, l_st2, p_st2,
            w_recv, w_send, w_fwd, gl_recv, gl_send, gn_recv, gn_send, t_recv, t_send,
-           n_recv, n_send, r_recv, r_send, l_recv, l_send, p_recv, p_send):
+           n_recv, n_send, r_recv, r_send, l_recv, l_send, p_recv, p_send,
+           w2_recv, w2_send, w2_fwd, gl2_recv, gl2_send, gn2_recv, gn2_send, l2_send, p2_send):
     r, d = out_ref.shape
     h = d // 2
     cw = h // nch
@@ -47,15 +48,35 @@
             pl.semaphore_signal(barrier, inc=1, device_id=(lax.rem(l + dl, nl), 2 * b + q), device_id_type=MESH)
     pl.semaphore_signal(barrier, inc=1, device_id=swap_mate, device_id_type=MESH)
 
-    @pl.when(b > 0)
+    first_lent = nch - lent
+    is_end = (b == 0) | (b == nb - 1)
+    helps = (b == 1) | (b == nb - 2)
+    mate_b = jnp.where((b == 0) | (b == nb - 1), jnp.where(b == 0, 1, nb - 2), jnp.where(b == 1, 0, nb - 1))
+    if not lent:
+        is_end = helps = b < 0
+    paired = is_end | helps
+
+    def mate(layer, q):
+        return (layer, 2 * mate_b + q)
+
+    @pl.when(paired)
+    def _():
+        for dl in range(nl):
+            for q in range(2):
+                pl.semaphore_signal(barrier, inc=1, device_id=mate(dl, q), device_id_type=MESH)
+
+    low_plain = (b > 0) & jnp.logical_not(paired & (mate_b == b - 1))
+    high_plain = (b < nb - 1) & jnp.logical_not(paired & (mate_b == b + 1))
+
+    @pl.when(low_plain)
     def _():
         pl.semaphore_signal(barrier, inc=1, device_id=(l, f - 2), device_id_type=MESH)
 
-    @pl.when(b < nb - 1)
+    @pl.when(high_plain)
     def _():
         pl.semaphore_signal(barrier, inc=1, device_id=(l, f + 2), device_id_type=MESH)
 
-    peers = 2 * nl - 1 + jnp.where(b > 0, 1, 0) + jnp.where(b < nb - 1, 1, 0)
+    peers = 2 * nl - 1 + jnp.where(paired, 2 * nl, 0) + jnp.where(low_plain, 1, 0) + jnp.where(high_plain, 1, 0)
     pl.semaphore_wait(barrier, peers)
 
     low = l + nl - 1
@@ -121,46 +142,59 @@
         @pl.when(home)
         def _():
             remote(w.at[m, 1 - p], w.at[m, 1 - p], w_fwd.at[m], w_recv.at[m, 1 - p], core_mate).start()
-        arrived(w.at[m, p], w_recv.at[m, p])
+        waited = home & is_end
+
+        @pl.when(jnp.logical_not(waited))
+        def _():
+            arrived(w.at[m, p], w_recv.at[m, p])
 
     def hop(buf, k, src, up, send, recv):
         dev = (l, f + 2) if up else (l, f - 2)
         return remote(buf.at[k, src], buf.at[k, src], send.at[k, src, 0 if up else 1], recv.at[k, src], dev)
 
+    def is_lent(k):
+        return k >= first_lent
+
+    def takes_part(k):
+        return jnp.logical_not(is_lent(k) & is_end)
+
+    def goes_up(k):
+        return (b < nb - 1) & takes_part(k) & jnp.logical_not(is_lent(k) & (b + 1 == nb - 1))
+
+    def goes_down(k):
+        return (b > 0) & takes_part(k) & jnp.logical_not(is_lent(k) & (b - 1 == 0))
+
+    def made_here(k, src):
+        return is_lent(k) & helps & (src == mate_b)
+
     def pass_on(buf, send, recv, live, k, j):
-        ok = live & (k >= 0) & (k < nch)
+        ok = live & (k >= 0) & (k < nch) & takes_part(k)
         if j == 0:
-            @pl.when(ok & (b < nb - 1))
+            @pl.when(ok & goes_up(k))
             def _():
                 hop(buf, k, b, True, send, recv).start()
 
-            @pl.when(ok & (b > 0))
+            @pl.when(ok & goes_down(k))
             def _():
                 hop(buf, k, b, False, send, recv).start()
         else:
-            @pl.when(ok & (b - j >= 0))
-            def _():
-                arrived(buf.at[k, b - j], recv.at[k, b - j])
-
-                @pl.when(b < nb - 1)
-                def _():
-                    hop(buf, k, b - j, True, send, recv).start()
-
-            @pl.when(ok & (b + j < nb))
-            def _():
-                arrived(buf.at[k, b + j], recv.at[k, b + j])
-
-                @pl.when(b > 0)
-                def _():
-                    hop(buf, k, b + j, False, send, recv).start()
+            for src, there, onward, up in ((b - j, b - j >= 0, goes_up(k), True),
+                                           (b + j, b + j < nb, goes_down(k), False)):
+                @pl.when(ok & there & jnp.logical_not(made_here(k, src)))
+                def _():
+                    arrived(buf.at[k, src], recv.at[k, src])
+
+                @pl.when(ok & there & onward)
+                def _():
+                    hop(buf, k, src, up, send, recv).start()
 
     def sent(buf, send, recv, live, k):
         for src in range(nb):
-            @pl.when(live & (src <= b) & (b < nb - 1))
+            @pl.when(live & (src <= b) & goes_up(k))
             def _():
                 hop(buf, k, src, True, send, recv).wait_send()
 
-            @pl.when(live & (src >= b) & (b > 0))
+            @pl.when(live & (src >= b) & goes_down(k))
             def _():
                 hop(buf, k, src, False, send, recv).wait_send()
 
@@ -169,23 +203,102 @@
 
     for i in range(2):
         arrived(tab.at[i], t_recv.at[i])
+
+    def near_of(x, k):
+        parts = [lax.dot_general(x[:, i * blk:(i + 1) * blk], tab[0, k * per + i],
+                                 (((1,), (1,)), ((), ())), preferred_element_type=F32).astype(BF)
+                 for i in range(per)]
+        return jnp.concatenate(parts, axis=1)
+
+    def lend_above(k):
+        return remote(gn.at[k], gn2.at[k - first_lent], gn2_send.at[k - first_lent],
+                      gn2_recv.at[k - first_lent], mate(l, p))
+
+    def lend_own():
+        cols = pl.ds(first_lent * cw, lent * cw)
+        return remote(gl.at[:, :, cols], gl2, gl2_send, gl2_recv, mate(l, p))
+
+    def lend_weight(m, q):
+        return remote(w.at[m, q], w2.at[m, q], w2_send.at[m, q], w2_recv.at[m, q], mate(l, p))
+
+    def share_weight(m, q):
+        return remote(w2.at[m, q], w2.at[m, q], w2_fwd.at[m, q], w2_recv.at[m, q], core_mate)
+
+    def take_lent(m):
+        for q in range(2):
+            arrived(w2.at[m, q], w2_recv.at[m, q])
+
+            @pl.when(home)
+            def _():
+                share_weight(m, q).start()
 
     def near_step(k):
         for q in range(2):
             arrived(gn.at[k, q], gn_recv.at[k, q])
-        x = gn[k].reshape(2 * r, cw)
-        parts = [lax.dot_general(x[:, i * blk:(i + 1) * blk], tab[0, k * per + i],
-                                 (((1,), (1,)), ((), ())), preferred_element_type=F32).astype(BF)
-                 for i in range(per)]
-        n_all[k, b] = jnp.concatenate(parts, axis=1)
+
+        @pl.when(takes_part(k))
+        def _():
+            n_all[k, b] = near_of(gn[k].reshape(2 * r, cw), k)
+
+        if lent:
+            @pl.when(jnp.logical_not(takes_part(k)))
+            def _():
+                lend_above(k).start()
+
+    def near_lent(k):
+        i = k - first_lent
+        arrived(gn2.at[i], gn2_recv.at[i])
+        n_all[k, mate_b] = near_of(gn2[i].reshape(2 * r, cw), k)
+
+    def reduced_lent(k):
+        cols = pl.ds(pl.multiple_of((k - first_lent) * cw, cw), cw)
+
+        @pl.when(k == first_lent)
+        def _():
+            arrived(gl2, gl2_recv)
+
+        @pl.when(chained)
+        def _():
+            x = n_all[k].reshape(nb * 2 * r, cw)
+            coupled = jnp.dot(w2[0].reshape(2 * r, d), x, preferred_element_type=F32)
+            r_all[k, mate_b] = (gl2[:, :, cols].reshape(2 * r, cw).astype(F32) - coupled).astype(BF)
+
+        @pl.when(jnp.logical_not(chained))
+        def _():
+            r_all[k, mate_b] = gl2[:, :, cols].reshape(2 * r, cw)
+
+    def local_lent(k, q):
+        i = k - first_lent
+        return remote(l_st2.at[i, q], l_in.at[k, c], l2_send.at[i, q], l_recv.at[k, c], mate(role, q))
+
+    def push_lent(k, q):
+        i = k - first_lent
+        return remote(p_st2.at[i, q], p_in.at[k, c], p2_send.at[i, q], p_recv.at[k, c],
+                      mate(lax.rem(role + 1, nl), q))
+
+    def final_lent(k):
+        i = k - first_lent
+        x = r_all[k].reshape(nb * 2 * r, cw)
+        white = jnp.dot(w2[1].reshape(2 * r, d), x, preferred_element_type=F32).astype(BF)
+        for n in range(per):
+            o = jnp.dot(white[:, n * blk:(n + 1) * blk], tab[1, k * per + n], preferred_element_type=F32)
+            l_st2[i, :, :, n * blk:(n + 1) * blk] = o.astype(BF).reshape(2, r, blk)
+        for q in range(2):
+            local_lent(k, q).start()
+
+        @pl.when(chained)
+        def _():
+            y = r_all[k].reshape(nb * 2 * r, cw)
+            carried = jnp.dot(w2[2].reshape(2 * r, d), y, preferred_element_type=F32).astype(BF)
+            for n in range(per):
+                mid = jnp.dot(carried[:, n * blk:(n + 1) * blk], tab[1, k * per + n],
+                              preferred_element_type=F32).astype(BF)
+                o = jnp.dot(mid, tab[0, k * per + n], preferred_element_type=F32)
+                p_st2[i, :, :, n * blk:(n + 1) * blk] = o.astype(BF).reshape(2, r, blk)
+            for q in range(2):
+                push_lent(k, q).start()
 
     def reduced_step(k):
-        @pl.when(k == 0)
-        def _():
-            for q in range(2):
-                arrived(gl.at[q], gl_recv.at[q])
-            take_weight(0)
-
         @pl.when(chained)
         def _():
             x = n_all[k].reshape(nb * 2 * r, cw)
@@ -264,28 +377,66 @@
         @pl.when(chained & inside(t))
         def _():
             near_step(t)
+        if lent:
+            @pl.when(chained & helps & inside(t - 1) & is_lent(t - 1))
+            def _():
+                near_lent(t - 1)
         for j in range(nb):
             pass_on(n_all, n_send, n_recv, chained, t - j, j)
         kr = t - n_lag
 
-        @pl.when(inside(kr))
+        @pl.when(kr == 0)
+        def _():
+            for q in range(2):
+                arrived(gl.at[q], gl_recv.at[q])
+            take_weight(0)
+        if lent:
+            @pl.when((kr == 0) & is_end)
+            def _():
+                lend_own().start()
+
+            @pl.when((kr == first_lent) & helps)
+            def _():
+                take_lent(0)
+
+        @pl.when(inside(kr) & takes_part(kr))
         def _():
             reduced_step(kr)
+        if lent:
+            @pl.when(helps & inside(kr - 1) & is_lent(kr - 1))
+            def _():
+                reduced_lent(kr - 1)
         for j in range(nb):
             pass_on(r_all, r_send, r_recv, True, kr - j, j)
 
-        @pl.when(kr == min(1, nch - 1))
-        def _():
-            take_weight(1)
-
-        @pl.when(kr == min(2, nch - 1))
-        def _():
-            take_weight(2)
+        for m in range(1, 3):
+            @pl.when(kr == min(m, nch - 1))
+            def _():
+                take_weight(m)
+        if lent:
+            for m in range(3):
+                @pl.when((t == m) & home & is_end)
+                def _():
+                    arrived(w.at[m, p], w_recv.at[m, p])
+                    lend_weight(m, p).start()
+
+                @pl.when((kr == m) & home & is_end)
+                def _():
+                    lend_weight(m, 1 - p).start()
+
+                if m:
+                    @pl.when((kr == first_lent + m) & helps)
+                    def _():
+                        take_lent(m)
         kf = t - r_lag
 
-        @pl.when(inside(kf))
+        @pl.when(inside(kf) & takes_part(kf))
         def _():
             final_step(kf)
+        if lent:
+            @pl.when(helps & inside(kf) & is_lent(kf))
+            def _():
+                final_lent(kf)
         ko = kf - 1
 
         @pl.when(inside(ko))
@@ -303,16 +454,42 @@
             def _():
                 above_copy(q, k).wait_send()
 
-            @pl.when(jnp.logical_not(stays(q, role)))
+            @pl.when(takes_part(k) & jnp.logical_not(stays(q, role)))
             def _():
                 local_copy(k, q).wait_send()
 
-            @pl.when(chained & jnp.logical_not(stays(q, role + 1)))
+            @pl.when(takes_part(k) & chained & jnp.logical_not(stays(q, role + 1)))
             def _():
                 push_copy(k, q).wait_send()
+
+            if lent:
+                @pl.when(is_lent(k) & helps)
+                def _():
+                    local_lent(k, q).wait_send()
+
+                @pl.when(is_lent(k) & helps & chained)
+                def _():
+                    push_lent(k, q).wait_send()
+        if lent:
+            @pl.when(chained & jnp.logical_not(takes_part(k)))
+            def _():
+                lend_above(k).wait_send()
         return carry
 
     lax.fori_loop(0, nch, drain, 0)
+    if lent:
+        @pl.when(is_end)
+        def _():
+            lend_own().wait_send()
+        for m in range(3):
+            for q in range(2):
+                @pl.when(home & is_end)
+                def _():
+                    lend_weight(m, q).wait_send()
+
+                @pl.when(home & helps)
+                def _():
+                    share_weight(m, q).wait_send()
 
     @pl.when(home)
     def _():
@@ -339,11 +516,13 @@
     hb = blocks // 2
     nch = hb // 2 if hb % 2 == 0 else hb
     cw = h // nch
+    lent = 2 if nb >= 4 and nch >= 5 else 0
+    keep = max(lent, 1)
     dma = pltpu.SemaphoreType.DMA
     vm = pltpu.VMEM
     anyspec = pl.BlockSpec(memory_space=pl.ANY)
     out = pl.pallas_call(
-        functools.partial(kernel, nl, nb, nch),
+        functools.partial(kernel, nl, nb, nch, lent),
         out_shape=jax.ShapeDtypeStruct((r, d), BF),
         in_specs=[anyspec] * 6,
         out_specs=pl.BlockSpec(memory_space=pltpu.VMEM),
@@ -351,9 +530,12 @@
             vm((3, 2, r, d), BF), vm((2, r, h), BF), vm((nch, 2, r, cw), BF), vm((2, hb, blk, blk), BF),
             vm((nch, nb, 2 * r, cw), BF), vm((nch, nb, 2 * r, cw), BF),
             vm((nch, 2, r, cw), BF), vm((nch, 2, r, cw), BF), vm((nch, 2, r, cw), BF), vm((nch, 2, r, cw), BF),
+            vm((3, 2, r, d), BF), vm((2, r, keep * cw), BF), vm((keep, 2, r, cw), BF),
+            vm((keep, 2, r, cw), BF), vm((keep, 2, r, cw), BF),
             dma((3, 2)), dma((3,)), dma((3,)), dma((2,)), dma((2,)), dma((nch, 2)), dma((nch, 2)), dma((2,)), dma((2,)),
             dma((nch, nb)), dma((nch, nb, 2)), dma((nch, nb)), dma((nch, nb, 2)),
             dma((nch, 2)), dma((nch, 2)), dma((nch, 2)), dma((nch, 2)),
+            dma((3, 2)), dma((3, 2)), dma((3, 2)), dma, dma, dma((keep,)), dma((keep,)), dma((keep, 2)), dma((keep, 2)),
         ],
         compiler_params=pltpu.CompilerParams(
             collective_id=0, has_side_effects=True, vmem_limit_bytes=62 * 1024 * 1024),

time: 238 us -> 234 us (0.983)
  Pallas kernels: 234 us -> 229 us
    pallas_call x1, Pallas kernels: 234 us -> 229 us  [local(): pl.pallas_call(functools.partial(kernel, nl, nb, nch, lent), out_shape=ja...]
where the time goes in v3:
time: 234 us; the launch traced here: 232 us
  Pallas kernels  229 us (98%)
  local copies, waits for them, and re-layouts  2.7 us (1%)
    pallas_call x1, Pallas kernels, local(): pl.pallas_call(functools.partial(kernel, nl, nb, nch, lent), out_shape=ja...  229 us

profile of v3, /device:TPU:5, one launch (start us, length us, event | category | flops | bytes accessed | tf_op | source)
XLA Modules:
  0.0 231.8 jit_solution(12989006531187516793)
XLA Ops:
  0.0 229.1 %shard_map.64 = bf16[320,2560]{1,0:T(8,128)(2,1)} custom-call(bf16[320,2560]{1,0:T(8,128)(2,1)} %bitcast.8, bf16[320,2560]{1,0:T(8,128)(2,1)} %bitcast.9, bf16[320,2560]{1,0:T(8,128)(2,1)} %bitcast.10, bf16[320,2560]{1,0:T(8,128)(2,1)} %bitcast.11, bf16[20,128,128]{2,1,0:T(8,128)(2,1)} %bitcast.12, bf16[20,128,128]{2,1,0:T(8,128)(2,1)} %bitcast.13), custom_call_target="tpu_custom_call" | custom-call | tf_op jit(solution)/shard_map/pallas_call | solution.py:524
  229.1 2.7 %copy.8 = bf16[1,320,2560]{2,1,0:T(8,128)(2,1)} copy(bf16[1,320,2560]{2,1,0:T(8,128)(2,1)} %bitcast.7) | data formatting | bytes 3276800

commit v4 on v3

--- a/solution.py
+++ b/solution.py
@@ -409,26 +409,32 @@
         for j in range(nb):
             pass_on(r_all, r_send, r_recv, True, kr - j, j)
 
-        for m in range(1, 3):
-            @pl.when(kr == min(m, nch - 1))
-            def _():
-                take_weight(m)
         if lent:
             for m in range(3):
-                @pl.when((t == m) & home & is_end)
+                @pl.when((t == m + 2) & home & is_end)
                 def _():
                     arrived(w.at[m, p], w_recv.at[m, p])
                     lend_weight(m, p).start()
 
-                @pl.when((kr == m) & home & is_end)
+                if m == 0:
+                    @pl.when((kr == 0) & home & is_end)
+                    def _():
+                        lend_weight(m, 1 - p).start()
+        kf = t - r_lag
+
+        @pl.when(kf == 0)
+        def _():
+            take_weight(1)
+            take_weight(2)
+        if lent:
+            for m in range(1, 3):
+                @pl.when((kf == 0) & home & is_end)
                 def _():
                     lend_weight(m, 1 - p).start()
 
-                if m:
-                    @pl.when((kr == first_lent + m) & helps)
-                    def _():
-                        take_lent(m)
-        kf = t - r_lag
+                @pl.when((kf == first_lent) & helps)
+                def _():
+                    take_lent(m)
 
         @pl.when(inside(kf) & takes_part(kf))
         def _():
@@ -516,7 +522,7 @@
     hb = blocks // 2
     nch = hb // 2 if hb % 2 == 0 else hb
     cw = h // nch
-    lent = 2 if nb >= 4 and nch >= 5 else 0
+    lent = 1 if nb >= 4 and nch >= 5 else 0
     keep = max(lent, 1)
     dma = pltpu.SemaphoreType.DMA
     vm = pltpu.VMEM

time: 234 us -> 218 us (0.932)
  Pallas kernels: 229 us -> 215 us
    pallas_call x1, Pallas kernels: 229 us -> 215 us  [local(): pl.pallas_call(functools.partial(kernel, nl, nb, nch, lent), out_shape=ja...]
where the time goes in v4:
time: 218 us
  Pallas kernels  215 us (99%)
  local copies, waits for them, and re-layouts  2.7 us (1%)
    pallas_call x1, Pallas kernels, local(): pl.pallas_call(functools.partial(kernel, nl, nb, nch, lent), out_shape=ja...  215 us

profile of v4, /device:TPU:5, one launch (start us, length us, event | category | flops | bytes accessed | tf_op | source)
XLA Modules:
  0.0 217.8 jit_solution(8643522430060281869)
XLA Ops:
  0.0 215.1 %shard_map.64 = bf16[320,2560]{1,0:T(8,128)(2,1)} custom-call(bf16[320,2560]{1,0:T(8,128)(2,1)} %bitcast.8, bf16[320,2560]{1,0:T(8,128)(2,1)} %bitcast.9, bf16[320,2560]{1,0:T(8,128)(2,1)} %bitcast.10, bf16[320,2560]{1,0:T(8,128)(2,1)} %bitcast.11, bf16[20,128,128]{2,1,0:T(8,128)(2,1)} %bitcast.12, bf16[20,128,128]{2,1,0:T(8,128)(2,1)} %bitcast.13), custom_call_target="tpu_custom_call" | custom-call | tf_op jit(solution)/shard_map/pallas_call | solution.py:530
  215.1 2.7 %copy.8 = bf16[1,320,2560]{2,1,0:T(8,128)(2,1)} copy(bf16[1,320,2560]{2,1,0:T(8,128)(2,1)} %bitcast.7) | data formatting | bytes 3276800

commit v5 on v4

--- a/solution.py
+++ b/solution.py
@@ -436,13 +436,14 @@
                 def _():
                     take_lent(m)
 
+        if lent:
+            @pl.when(helps & inside(kf) & is_lent(kf))
+            def _():
+                final_lent(kf)
+
         @pl.when(inside(kf) & takes_part(kf))
         def _():
             final_step(kf)
-        if lent:
-            @pl.when(helps & inside(kf) & is_lent(kf))
-            def _():
-                final_lent(kf)
         ko = kf - 1
 
         @pl.when(inside(ko))

time: 218 us -> 215 us (0.986)
  Pallas kernels: 215 us -> 212 us
    pallas_call x1, Pallas kernels: 215 us -> 212 us  [local(): pl.pallas_call(functools.partial(kernel, nl, nb, nch, lent), out_shape=ja...]
where the time goes in v5:
time: 215 us
  Pallas kernels  212 us (99%)
  local copies, waits for them, and re-layouts  2.7 us (1%)
    pallas_call x1, Pallas kernels, local(): pl.pallas_call(functools.partial(kernel, nl, nb, nch, lent), out_shape=ja...  212 us

profile of v5, /device:TPU:5, one launch (start us, length us, event | category | flops | bytes accessed | tf_op | source)
XLA Modules:
  0.0 214.6 jit_solution(16246616307350558431)
XLA Ops:
  0.0 211.9 %shard_map.64 = bf16[320,2560]{1,0:T(8,128)(2,1)} custom-call(bf16[320,2560]{1,0:T(8,128)(2,1)} %bitcast.8, bf16[320,2560]{1,0:T(8,128)(2,1)} %bitcast.9, bf16[320,2560]{1,0:T(8,128)(2,1)} %bitcast.10, bf16[320,2560]{1,0:T(8,128)(2,1)} %bitcast.11, bf16[20,128,128]{2,1,0:T(8,128)(2,1)} %bitcast.12, bf16[20,128,128]{2,1,0:T(8,128)(2,1)} %bitcast.13), custom_call_target="tpu_custom_call" | custom-call | tf_op jit(solution)/shard_map/pallas_call | solution.py:531
  211.9 2.7 %copy.8 = bf16[1,320,2560]{2,1,0:T(8,128)(2,1)} copy(bf16[1,320,2560]{2,1,0:T(8,128)(2,1)} %bitcast.7) | data formatting | bytes 3276800
